TPU v7x, 32 devices: a whole 2x2x4 slice. The times are simulated.
32 devices in a mesh: row: 8 (over y, x, core), col: 4 (over z).
Axes of the slice: x: 2, y: 2, z: 4, core: 2. Of those that a mesh axis runs over, the one named last changes fastest.
Arguments:
- tokens: bfloat16 [4, 4096, 1792], P(None, ('row', 'col')), may hold values from -12 to 12
- lengths: int32 [4, 8], replicated, may hold values from 1 to 1024, 4096 in all within a row
- permutation: int32 [4, 32], replicated, may hold values from 0 to 31, each once within a row
- cotangent: bfloat16 [4, 4096, 1792], P(None, ('row', 'col')), may hold values from -12 to 12
- norm1_gain: float32 [1792], replicated, may hold values from 0.5 to 1.5
- mixer_in: bfloat16 [1792, 1792], P('row', 'col'), may hold values from -0.125 to 0.125
- mixer_gate: bfloat16 [1792, 1792], P('row', 'col'), may hold values from -0.125 to 0.125
- conv_kernel: float32 [3, 1792], P(None, 'col'), may hold values from -2.5 to 2.5
- mixer_out: bfloat16 [1792, 1792], P('row', 'col'), may hold values from -0.125 to 0.125
- norm2_gain: float32 [1792], replicated, may hold values from 0.5 to 1.5
- ffn_gate: bfloat16 [1792, 4864], P('row', 'col'), may hold values from -0.125 to 0.125
- ffn_up: bfloat16 [1792, 4864], P('row', 'col'), may hold values from -0.125 to 0.125
- ffn_down: bfloat16 [1792, 4864], P('row', 'col'), may hold values from -0.078125 to 0.078125
Outputs:
- output: bfloat16 [4, 4096, 1792], P(None, ('row', 'col'))
- input_grad: float32 [4, 4096, 1792], P(None, ('row', 'col'))
- norm1_gain_grad: float32 [1792], P(('row', 'col'))
- mixer_in_grad: float32 [1792, 1792], P('row', 'col')
- mixer_gate_grad: float32 [1792, 1792], P('row', 'col')
- conv_kernel_grad: float32 [3, 1792], P(None, ('col', 'row'))
- mixer_out_grad: float32 [1792, 1792], P('row', 'col')
- norm2_gain_grad: float32 [1792], P(('row', 'col'))
- ffn_gate_grad: float32 [1792, 4864], P('row', 'col')
- ffn_up_grad: float32 [1792, 4864], P('row', 'col')
- ffn_down_grad: float32 [1792, 4864], P('row', 'col')
Inputs may be any that keep to these rules, and one draw needn't show every extreme that they name: Each row of lengths sums to 4096, and its largest entry is exactly 1024. `permutation`: each row holds every number of 0 to 31 once.
All inputs are finite; a program needn't handle non-finite values.
Results may differ from a plain program's by a relative error of at most 0.0083.
Values may be sent and summed in bfloat16 or wider, within the bound.
No kernel may reach another device: no remote copies, remote signals or barrier semaphores. Data moves between devices by JAX's collectives and lax.ppermute only.
A program may use at most 160 MiB of HBM per device.

v0:
```python
import jax
import jax.numpy as jnp
from jax import lax
from jax.sharding import PartitionSpec as P

BLOCK = 128
EPSILON = 1e-05


def contract_last(left, right):
    return lax.dot_general(
        left, right, (((1,), (1,)), ((), ())), preferred_element_type=jnp.float32
    )


def contract_first(left, right):
    return lax.dot_general(
        left, right, (((0,), (0,)), ((), ())), preferred_element_type=jnp.float32
    )


def spread(shard):
    return lax.all_gather(shard, "col", axis=0, tiled=True)


def spread_grad(shard):
    return lax.all_gather(shard, "col", axis=0, tiled=True)


def collect(partial_sum):
    return lax.psum_scatter(partial_sum, "col", scatter_dimension=0, tiled=True)


def collect_grad(partial_sum):
    return lax.psum_scatter(partial_sum, "col", scatter_dimension=0, tiled=True)


def per_device(
    tokens,
    lengths,
    permutation,
    cotangent,
    norm1_gain,
    mixer_in,
    mixer_gate,
    conv_kernel,
    mixer_out,
    norm2_gain,
    ffn_gate,
    ffn_up,
    ffn_down,
):
    micro_count, rows_local, full_width = tokens.shape
    group_rows = rows_local * lax.axis_size("col")
    block_size = BLOCK
    blocks_local = group_rows // block_size
    blocks_all = permutation.shape[1]
    row_index = lax.axis_index("row")
    width_local = conv_kernel.shape[1]
    within = jnp.arange(block_size, dtype=jnp.int32)
    blocks_range = jnp.arange(blocks_all, dtype=jnp.int32)
    outputs = []
    input_grads = []
    totals = None
    for micro_index in range(micro_count):
        gathered = (
            lax.all_gather(mixer_in, "row", axis=0, tiled=True),
            lax.all_gather(mixer_gate, "row", axis=0, tiled=True),
            lax.all_gather(ffn_gate, "row", axis=0, tiled=True),
            lax.all_gather(ffn_up, "row", axis=0, tiled=True),
            lax.all_gather(mixer_out, "row", axis=0, tiled=True),
            lax.all_gather(ffn_down, "row", axis=0, tiled=True),
        )
        w_in, w_gate, w_ffg, w_ffu, w_out, w_down = gathered
        local_in = tokens[micro_index].astype(jnp.float32)
        local_cot = cotangent[micro_index]
        dealt_order = permutation[micro_index]
        seq_len = lengths[micro_index]
        offsets = jnp.cumsum(seq_len) - seq_len
        own_blocks = lax.dynamic_slice_in_dim(dealt_order, row_index * blocks_local, blocks_local)
        inverse = jnp.sum(
            jnp.where(dealt_order[None, :] == blocks_range[:, None], blocks_range[None, :], 0),
            axis=1,
        )
        source = jnp.take(inverse, jnp.maximum(own_blocks - 1, 0))
        position = (own_blocks[:, None] * block_size + within[None, :]).reshape(-1)
        is_start = jnp.any(position[:, None] == offsets[None, :], axis=1)
        was_start = jnp.any(position[:, None] - 1 == offsets[None, :], axis=1)
        keep_one = jnp.where(is_start, 0.0, 1.0).astype(jnp.float32)[:, None]
        keep_two = jnp.where(is_start | was_start, 0.0, 1.0).astype(jnp.float32)[:, None]
        scale_one = lax.rsqrt(jnp.mean(local_in * local_in, axis=1, keepdims=True) + EPSILON)
        normed_one = local_in * scale_one
        hidden_one = spread((normed_one * norm1_gain).astype(jnp.bfloat16))
        signal = jnp.dot(hidden_one, w_in, preferred_element_type=jnp.float32)
        gating = jnp.dot(hidden_one, w_gate, preferred_element_type=jnp.float32)
        signal_blocks = signal.reshape(blocks_local, block_size, width_local)
        tails_all = lax.all_gather(signal_blocks[:, block_size - 2 :, :], "row", axis=0, tiled=True)
        before = jnp.take(tails_all, source, axis=0)
        extended = jnp.concatenate([before, signal_blocks], axis=1)
        shift_one = keep_one * extended[:, 1 : block_size + 1, :].reshape(group_rows, width_local)
        shift_two = keep_two * extended[:, 0:block_size, :].reshape(group_rows, width_local)
        mixed_sig = (
            conv_kernel[0] * signal + conv_kernel[1] * shift_one + conv_kernel[2] * shift_two
        )
        product = (mixed_sig * gating).astype(jnp.bfloat16)
        branch = collect(contract_last(product, w_out))
        residual = local_in + branch
        scale_two = lax.rsqrt(jnp.mean(residual * residual, axis=1, keepdims=True) + EPSILON)
        normed_two = residual * scale_two
        hidden_two = spread((normed_two * norm2_gain).astype(jnp.bfloat16))
        gate_val = jnp.dot(hidden_two, w_ffg, preferred_element_type=jnp.float32)
        up_val = jnp.dot(hidden_two, w_ffu, preferred_element_type=jnp.float32)
        sigmoid_gate = jax.nn.sigmoid(gate_val)
        activated = (gate_val * sigmoid_gate * up_val).astype(jnp.bfloat16)
        ffn_result = collect(contract_last(activated, w_down))
        outputs.append((residual + ffn_result).astype(jnp.bfloat16))
        grad_full = spread_grad(local_cot)
        grad_act = jnp.dot(grad_full, w_down, preferred_element_type=jnp.float32)
        grad_down = contract_first(grad_full, activated)
        silu_slope = sigmoid_gate * (1.0 + gate_val * (1.0 - sigmoid_gate))
        grad_gate = (grad_act * up_val * silu_slope).astype(jnp.bfloat16)
        grad_up = (grad_act * gate_val * sigmoid_gate).astype(jnp.bfloat16)
        grad_ffg = contract_first(hidden_two, grad_gate)
        grad_ffu = contract_first(hidden_two, grad_up)
        grad_hidden_two = collect_grad(
            contract_last(grad_gate, w_ffg) + contract_last(grad_up, w_ffu)
        )
        grad_gain_two = jnp.sum(grad_hidden_two * normed_two, axis=0)
        grad_norm_two = grad_hidden_two * norm2_gain
        inner_two = jnp.mean(grad_norm_two * normed_two, axis=1, keepdims=True)
        grad_residual = local_cot.astype(jnp.float32) + scale_two * (
            grad_norm_two - normed_two * inner_two
        )
        grad_branch = spread_grad(grad_residual.astype(jnp.bfloat16))
        grad_product = jnp.dot(grad_branch, w_out, preferred_element_type=jnp.float32)
        grad_out_w = contract_first(grad_branch, product)
        grad_mixed = grad_product * gating
        grad_gating = (grad_product * mixed_sig).astype(jnp.bfloat16)
        grad_kernel = jnp.stack(
            [
                jnp.sum(grad_mixed * signal, axis=0),
                jnp.sum(grad_mixed * shift_one, axis=0),
                jnp.sum(grad_mixed * shift_two, axis=0),
            ]
        )
        into_one = (conv_kernel[1] * keep_one * grad_mixed).reshape(
            blocks_local, block_size, width_local
        )
        into_two = (conv_kernel[2] * keep_two * grad_mixed).reshape(
            blocks_local, block_size, width_local
        )
        grad_extended = jnp.pad(into_one, ((0, 0), (1, 1), (0, 0))) + jnp.pad(
            into_two, ((0, 0), (0, 2), (0, 0))
        )
        grad_before = grad_extended[:, :2, :]
        grad_blocks = grad_extended[:, 2:, :] + (conv_kernel[0] * grad_mixed).reshape(
            blocks_local, block_size, width_local
        )
        chooser = (source[:, None] == blocks_range[None, :]).astype(jnp.float32)
        tail_terms = jnp.einsum("jn,jtd->ntd", chooser, grad_before)
        returned = lax.psum_scatter(
            tail_terms.astype(jnp.bfloat16), "row", scatter_dimension=0, tiled=True
        ).astype(jnp.float32)
        grad_blocks = jnp.concatenate(
            [grad_blocks[:, : block_size - 2, :], grad_blocks[:, block_size - 2 :, :] + returned],
            axis=1,
        )
        grad_signal = grad_blocks.reshape(group_rows, width_local).astype(jnp.bfloat16)
        grad_in_w = contract_first(hidden_one, grad_signal)
        grad_gate_w = contract_first(hidden_one, grad_gating)
        grad_hidden_one = collect_grad(
            contract_last(grad_signal, w_in) + contract_last(grad_gating, w_gate)
        )
        grad_gain_one = jnp.sum(grad_hidden_one * normed_one, axis=0)
        grad_norm_one = grad_hidden_one * norm1_gain
        inner_one = jnp.mean(grad_norm_one * normed_one, axis=1, keepdims=True)
        input_grads.append(grad_residual + scale_one * (grad_norm_one - normed_one * inner_one))
        partials = (
            grad_gain_one,
            grad_in_w,
            grad_gate_w,
            grad_kernel,
            grad_out_w,
            grad_gain_two,
            grad_ffg,
            grad_ffu,
            grad_down,
        )
        partials = (
            lax.psum_scatter(partials[0], "row", scatter_dimension=0, tiled=True),
            lax.psum_scatter(partials[1], "row", scatter_dimension=0, tiled=True),
            lax.psum_scatter(partials[2], "row", scatter_dimension=0, tiled=True),
            lax.psum_scatter(partials[3], "row", scatter_dimension=1, tiled=True),
            lax.psum_scatter(partials[4], "row", scatter_dimension=0, tiled=True),
            lax.psum_scatter(partials[5], "row", scatter_dimension=0, tiled=True),
            lax.psum_scatter(partials[6], "row", scatter_dimension=0, tiled=True),
            lax.psum_scatter(partials[7], "row", scatter_dimension=0, tiled=True),
            lax.psum_scatter(partials[8], "row", scatter_dimension=0, tiled=True),
        )
        if totals is None:
            totals = tuple(partials)
        else:
            totals = tuple((left_val + right_val for left_val, right_val in zip(totals, partials)))
    gain_one_total, gain_two_total = (
        lax.psum_scatter(totals[0], "col", scatter_dimension=0, tiled=True),
        lax.psum_scatter(totals[5], "col", scatter_dimension=0, tiled=True),
    )
    return (
        jnp.stack(outputs),
        jnp.stack(input_grads),
        gain_one_total,
        totals[1],
        totals[2],
        totals[3],
        totals[4],
        gain_two_total,
        totals[6],
        totals[7],
        totals[8],
    )


def solution(mesh):
    placed = (
        P(None, ("row", "col"), None),
        P(),
        P(),
        P(None, ("row", "col"), None),
        P(),
        P("row", "col"),
        P("row", "col"),
        P(None, "col"),
        P("row", "col"),
        P(),
        P("row", "col"),
        P("row", "col"),
        P("row", "col"),
    )
    return jax.shard_map(
        per_device,
        mesh=mesh,
        in_specs=placed,
        out_specs=(
            P(None, ("row", "col"), None),
            P(None, ("row", "col"), None),
            P(("row", "col")),
            P("row", "col"),
            P("row", "col"),
            P(None, ("col", "row")),
            P("row", "col"),
            P(("row", "col")),
            P("row", "col"),
            P("row", "col"),
            P("row", "col"),
        ),
        check_vma=False,
    )
```

profile of v0, /device:TPU:0, one launch (start us, length us, event | category | flops | bytes accessed | tf_op | source)
XLA Modules:
  0.0 2552.2 jit_solution(138353777836643099)
XLA Ops:
  18.1 37.2 %all-gather.27.cloned.1.call-done = bf16[512,1792]{1,0:T(8,128)(2,1)} async-done(((bf16[128,1792]{1,0:T(8,128)(2,1)}), bf16[512,1792]{1,0:T(8,128)(2,1)}) %all-gather.27.cloned.1.call-update) | async-done | bytes 1835024 | tf_op jit(solution)/shard_map/all_gather | solution.py:23
  338.3 71.1 %reduce-scatter.38.cloned.1.call-done = f32[128,1792]{1,0:T(8,128)} async-done(((f32[512,1792]{1,0:T(8,128)}), f32[128,1792]{1,0:T(8,128)}) %reduce-scatter.38.cloned.1.call-update) | async-done | bytes 917520 | tf_op jit(solution)/shard_map/reduce_scatter | solution.py:31
  409.4 71.0 %reduce-scatter.42.cloned.1.call-done = f32[128,1792]{1,0:T(8,128)} async-done(((f32[512,1792]{1,0:T(8,128)}), f32[128,1792]{1,0:T(8,128)}) %reduce-scatter.42.cloned.1.call-update) | async-done | bytes 917520 | tf_op jit(solution)/shard_map/reduce_scatter | solution.py:31
  480.4 71.1 %reduce-scatter.34.cloned.1.call-done = f32[128,1792]{1,0:T(8,128)} async-done(((f32[512,1792]{1,0:T(8,128)}), f32[128,1792]{1,0:T(8,128)}) %reduce-scatter.34.cloned.1.call-update) | async-done | bytes 917520 | tf_op jit(solution)/shard_map/reduce_scatter | solution.py:31
  592.0 43.6 %all-gather.49.cloned.1.call-done = bf16[512,1792]{1,0:T(8,128)(2,1)} async-done(((bf16[128,1792]{1,0:T(8,128)(2,1)}), bf16[512,1792]{1,0:T(8,128)(2,1)}) %all-gather.49.cloned.1.call-update) | async-done | bytes 1835024 | tf_op jit(solution)/shard_map/all_gather | solution.py:23
  717.4 39.0 %all-gather.41.cloned.1.call-done = bf16[1792,1216]{1,0:T(8,128)(2,1)} async-done(((bf16[224,1216]{1,0:T(8,128)(2,1)}), bf16[1792,1216]{1,0:T(8,128)(2,1)}) %all-gather.41.cloned.1.call-update) | async-done | bytes 4358160 | tf_op jit(solution)/shard_map/all_gather | solution.py:72
  863.7 48.1 %reduce-scatter.54.cloned.1.call-done = f32[128,1792]{1,0:T(8,128)} async-done(((f32[512,1792]{1,0:T(8,128)}), f32[128,1792]{1,0:T(8,128)}) %reduce-scatter.54.cloned.1.call-update) | async-done | bytes 917520 | tf_op jit(solution)/shard_map/reduce_scatter | solution.py:35
  911.8 71.0 %reduce-scatter.46.cloned.1.call-done = f32[128,1792]{1,0:T(8,128)} async-done(((f32[512,1792]{1,0:T(8,128)}), f32[128,1792]{1,0:T(8,128)}) %reduce-scatter.46.cloned.1.call-update) | async-done | bytes 917520 | tf_op jit(solution)/shard_map/reduce_scatter | solution.py:35
  989.2 39.8 %all-gather.45.cloned.1.call-done = bf16[512,1792]{1,0:T(8,128)(2,1)} async-done(((bf16[128,1792]{1,0:T(8,128)(2,1)}), bf16[512,1792]{1,0:T(8,128)(2,1)}) %all-gather.45.cloned.1.call-update) | async-done | bytes 1835024 | tf_op jit(solution)/shard_map/all_gather | solution.py:23
  1224.7 71.0 %reduce-scatter.58.cloned.1.call-done = f32[128,1792]{1,0:T(8,128)} async-done(((f32[512,1792]{1,0:T(8,128)}), f32[128,1792]{1,0:T(8,128)}) %reduce-scatter.58.cloned.1.call-update) | async-done | bytes 917520 | tf_op jit(solution)/shard_map/reduce_scatter | solution.py:35
  1300.2 66.5 %reduce-scatter.36.cloned.1.call-done = f32[128,1792]{1,0:T(8,128)} async-done(((f32[512,1792]{1,0:T(8,128)}), f32[128,1792]{1,0:T(8,128)}) %reduce-scatter.36.cloned.1.call-update) | async-done | bytes 917520 | tf_op jit(solution)/shard_map/reduce_scatter | solution.py:31
  1366.7 71.1 %reduce-scatter.44.cloned.1.call-done = f32[128,1792]{1,0:T(8,128)} async-done(((f32[512,1792]{1,0:T(8,128)}), f32[128,1792]{1,0:T(8,128)}) %reduce-scatter.44.cloned.1.call-update) | async-done | bytes 917520 | tf_op jit(solution)/shard_map/reduce_scatter | solution.py:31
  1447.2 38.1 %all-gather.61.cloned.1.call-done = bf16[512,1792]{1,0:T(8,128)(2,1)} async-done(((bf16[128,1792]{1,0:T(8,128)(2,1)}), bf16[512,1792]{1,0:T(8,128)(2,1)}) %all-gather.61.cloned.1.call-update) | async-done | bytes 1835024 | tf_op jit(solution)/shard_map/all_gather | solution.py:27
  1532.5 36.5 %all-gather.59.cloned.1.call-done = bf16[512,1792]{1,0:T(8,128)(2,1)} async-done(((bf16[128,1792]{1,0:T(8,128)(2,1)}), bf16[512,1792]{1,0:T(8,128)(2,1)}) %all-gather.59.cloned.1.call-update) | async-done | bytes 1835024 | tf_op jit(solution)/shard_map/all_gather | solution.py:27
  1574.8 36.6 %all-gather.55.cloned.1.call-done = bf16[512,1792]{1,0:T(8,128)(2,1)} async-done(((bf16[128,1792]{1,0:T(8,128)(2,1)}), bf16[512,1792]{1,0:T(8,128)(2,1)}) %all-gather.55.cloned.1.call-update) | async-done | bytes 1835024 | tf_op jit(solution)/shard_map/all_gather | solution.py:27
  1666.5 49.7 %all-reduce.22.cloned.1.call-done = (bf16[32,2,448]{2,0,1:T(8,128)(2,1)}, bf16[32,2,448]{2,0,1:T(8,128)(2,1)}, bf16[32,2,448]{2,0,1:T(8,128)(2,1)}, bf16[32,2,448]{2,0,1:T(8,128)(2,1)}) async-done(((bf16[32,2,448]{2,0,1:T(8,128)(2,1)}, bf16[32,2,448]{2,0,1:T(8,128)(2,1)}, bf16[32,2,448]{2,0,1:T(8,128)(2,1)}, bf16[32,2,448]{2,0,1:T(8,128)(2,1)}), (bf16[32,2,448]{2,0,1:T(8,128)(2,1)}, ...) | async-done | bytes 229392
  1934.3 71.1 %reduce-scatter.48.cloned.1.call-done = f32[128,1792]{1,0:T(8,128)} async-done(((f32[512,1792]{1,0:T(8,128)}), f32[128,1792]{1,0:T(8,128)}) %reduce-scatter.48.cloned.1.call-update) | async-done | bytes 917520 | tf_op jit(solution)/shard_map/reduce_scatter | solution.py:35
  2080.5 67.4 %reduce-scatter.32.cloned.1.call-done = f32[128,1792]{1,0:T(8,128)} async-done(((f32[512,1792]{1,0:T(8,128)}), f32[128,1792]{1,0:T(8,128)}) %reduce-scatter.32.cloned.1.call-update) | async-done | bytes 917520 | tf_op jit(solution)/shard_map/reduce_scatter | solution.py:31
  2158.3 69.7 %reduce-scatter.68.cloned.1.call-done = f32[224,1216]{1,0:T(8,128)} async-done(((f32[1792,1216]{1,0:T(8,128)}), f32[224,1216]{1,0:T(8,128)}) %reduce-scatter.68.cloned.1.call-update) | async-done | bytes 1089552 | tf_op jit(solution)/shard_map/reduce_scatter | solution.py:196
  2228.0 79.3 %reduce-scatter.70.cloned.1.call-done = f32[224,1216]{1,0:T(8,128)} async-done(((f32[1792,1216]{1,0:T(8,128)}), f32[224,1216]{1,0:T(8,128)}) %reduce-scatter.70.cloned.1.call-update) | async-done | bytes 1089552 | tf_op jit(solution)/shard_map/reduce_scatter | solution.py:197
  2307.3 79.7 %reduce-scatter.72.cloned.1.call-done = f32[224,1216]{1,0:T(8,128)} async-done(((f32[1792,1216]{1,0:T(8,128)}), f32[224,1216]{1,0:T(8,128)}) %reduce-scatter.72.cloned.1.call-update) | async-done | bytes 1089552
  2387.0 52.6 %reduce-scatter.64.cloned.1.call-done = f32[224,448]{1,0:T(8,128)} async-done(((f32[1792,448]{1,0:T(8,128)}), f32[224,448]{1,0:T(8,128)}) %reduce-scatter.64.cloned.1.call-update) | async-done | bytes 401424 | tf_op jit(solution)/shard_map/reduce_scatter | solution.py:192
  2439.6 53.2 %reduce-scatter.66.cloned.1.call-done = f32[224,448]{1,0:T(8,128)} async-done(((f32[1792,448]{1,0:T(8,128)}), f32[224,448]{1,0:T(8,128)}) %reduce-scatter.66.cloned.1.call-update) | async-done | bytes 401424 | tf_op jit(solution)/shard_map/reduce_scatter | solution.py:194
  2492.8 52.6 %reduce-scatter.62.cloned.1.call-done = f32[224,448]{1,0:T(8,128)} async-done(((f32[1792,448]{1,0:T(8,128)}), f32[224,448]{1,0:T(8,128)}) %reduce-scatter.62.cloned.1.call-update) | async-done | bytes 401424 | tf_op jit(solution)/shard_map/reduce_scatter | solution.py:191
  (724 shorter events, 1145.8 us)
Async XLA Ops:
  13.6 212.6 %all-gather.47.cloned.1.call-start = ((), (), s32[]{:S(2)}) async-start(), calls=%async_computation.36 | async-start | bytes 2293760 | tf_op jit(solution)/shard_map/all_gather | solution.py:23
  14.2 253.9 %all-gather.51.cloned.1.call-start = ((), (), s32[]{:S(2)}) async-start(), calls=%async_computation.40 | async-start | bytes 2293760 | tf_op jit(solution)/shard_map/all_gather | solution.py:23
  15.0 323.3 %reduce-scatter.30.cloned.1.call-start = ((), (), s32[]{:S(2)}) async-start(), calls=%async_computation.26 | async-start | bytes 4587520 | tf_op jit(solution)/shard_map/reduce_scatter | solution.py:31
  187.5 221.9 %reduce-scatter.38.cloned.1.call-start = ((), (), s32[]{:S(2)}) async-start(), calls=%async_computation.37 | async-start | bytes 4587520 | tf_op jit(solution)/shard_map/reduce_scatter | solution.py:31
  310.0 241.5 %reduce-scatter.34.cloned.1.call-start = ((), (), s32[]{:S(2)}) async-start(), calls=%async_computation.33 | async-start | bytes 4587520 | tf_op jit(solution)/shard_map/reduce_scatter | solution.py:31
  313.1 278.9 %all-gather.37.cloned.1.call-start = ((), (), s32[]{:S(2)}) async-start(), calls=%async_computation.28 | async-start | bytes 5160960 | tf_op jit(solution)/shard_map/all_gather | solution.py:69
  313.7 321.9 %all-gather.49.cloned.1.call-start = ((), (), s32[]{:S(2)}) async-start(), calls=%async_computation.38 | async-start | bytes 2293760 | tf_op jit(solution)/shard_map/all_gather | solution.py:23
  561.9 238.0 %all-gather.35.cloned.1.call-start = ((), (), s32[]{:S(2)}) async-start(), calls=%async_computation.27 | async-start | bytes 2293760 | tf_op jit(solution)/shard_map/all_gather | solution.py:23
  562.5 279.1 %all-gather.63.cloned.1.call-start = ((), (), s32[]{:S(2)}) async-start(), calls=%async_computation.56 | async-start | bytes 2293760 | tf_op jit(solution)/shard_map/all_gather | solution.py:27
  563.0 348.7 %reduce-scatter.54.cloned.1.call-start = ((), (), s32[]{:S(2)}) async-start(), calls=%async_computation.50 | async-start | bytes 4587520 | tf_op jit(solution)/shard_map/reduce_scatter | solution.py:35
  989.2 235.5 %reduce-scatter.50.cloned.1.call-start = ((), (), s32[]{:S(2)}) async-start(), calls=%async_computation.47 | async-start | bytes 4587520 | tf_op jit(solution)/shard_map/reduce_scatter | solution.py:35
  1183.6 254.2 %reduce-scatter.44.cloned.1.call-start = ((), (), s32[]{:S(2)}) async-start(), calls=%async_computation.43 | async-start | bytes 4587520 | tf_op jit(solution)/shard_map/reduce_scatter | solution.py:31
  1190.9 294.5 %all-gather.61.cloned.1.call-start = ((), (), s32[]{:S(2)}) async-start(), calls=%async_computation.54 | async-start | bytes 2293760 | tf_op jit(solution)/shard_map/all_gather | solution.py:27
  1445.5 270.7 %all-reduce.22.cloned.1.call-start = ((), (), s32[]{:S(2)}) async-start(), calls=%async_computation.66 | async-start | bytes 524288
  1663.1 246.5 %reduce-scatter.56.cloned.1.call-start = ((), (), s32[]{:S(2)}) async-start(), calls=%async_computation.52 | async-start | bytes 4587520 | tf_op jit(solution)/shard_map/reduce_scatter | solution.py:35
  1757.9 247.4 %reduce-scatter.48.cloned.1.call-start = ((), (), s32[]{:S(2)}) async-start(), calls=%async_computation.46 | async-start | bytes 4587520 | tf_op jit(solution)/shard_map/reduce_scatter | solution.py:35
  1772.8 304.0 %reduce-scatter.40.cloned.1.call-start = ((), (), s32[]{:S(2)}) async-start(), calls=%async_computation.39 | async-start | bytes 4587520 | tf_op jit(solution)/shard_map/reduce_scatter | solution.py:31
  1780.8 367.1 %reduce-scatter.32.cloned.1.call-start = ((), (), s32[]{:S(2)}) async-start(), calls=%async_computation.31 | async-start | bytes 4587520 | tf_op jit(solution)/shard_map/reduce_scatter | solution.py:31
  1788.8 439.2 %reduce-scatter.68.cloned.1.call-start = ((), (), s32[]{:S(2)}) async-start(), calls=%async_computation.63 | async-start | bytes 10321920 | tf_op jit(solution)/shard_map/reduce_scatter | solution.py:196
  1819.4 487.9 %reduce-scatter.70.cloned.1.call-start = ((), (), s32[]{:S(2)}) async-start(), calls=%async_computation.64 | async-start | bytes 10321920 | tf_op jit(solution)/shard_map/reduce_scatter | solution.py:197
  1849.6 537.4 %reduce-scatter.72.cloned.1.call-start = ((), (), s32[]{:S(2)}) async-start(), calls=%async_computation.65 | async-start | bytes 10321920
  1876.8 562.8 %reduce-scatter.64.cloned.1.call-start = ((), (), s32[]{:S(2)}) async-start(), calls=%async_computation.61 | async-start | bytes 4128768 | tf_op jit(solution)/shard_map/reduce_scatter | solution.py:192
  1886.8 606.0 %reduce-scatter.66.cloned.1.call-start = ((), (), s32[]{:S(2)}) async-start(), calls=%async_computation.62 | async-start | bytes 4128768 | tf_op jit(solution)/shard_map/reduce_scatter | solution.py:194
  1896.9 648.5 %reduce-scatter.62.cloned.1.call-start = ((), (), s32[]{:S(2)}) async-start(), calls=%async_computation.60 | async-start | bytes 4128768 | tf_op jit(solution)/shard_map/reduce_scatter | solution.py:191
  (205 other events, 11443.8 us)
Sparse Core Ops, SparseCore 0:
  11.1 44.0 all-gather.26
  270.9 67.2 reduce-scatter.29
  340.6 68.7 reduce-scatter.37
  411.5 68.7 reduce-scatter.41
  482.7 68.7 reduce-scatter.33
  844.5 67.2 reduce-scatter.53
  913.9 68.7 reduce-scatter.45
  1157.4 67.2 reduce-scatter.49
  1226.9 68.7 reduce-scatter.57
  1297.8 68.7 reduce-scatter.35
  1369.0 68.7 reduce-scatter.43
  1663.2 52.9 all-reduce.21
  1724.2 67.7 reduce-scatter.55
  1794.4 68.7 reduce-scatter.59
  1865.5 68.7 reduce-scatter.51
  1936.5 68.7 reduce-scatter.47
  2007.8 69.0 reduce-scatter.39
  2079.1 68.7 reduce-scatter.31
  2152.6 75.4 reduce-scatter.67
  2232.2 75.0 reduce-scatter.69
  2311.9 75.0 reduce-scatter.71
  2390.9 48.6 reduce-scatter.63
  2444.0 48.7 reduce-scatter.65
  2496.7 48.7 reduce-scatter.61
  (21 shorter events, 803.1 us)
where the time goes:
time: 2560 us; the launch traced here: 2550 us
  waiting for transfers between devices  1900 us (74%)
  matrix products  355 us (14%)
  local copies, waits for them, and re-layouts  126 us (5%)
  blocking collectives  74 us (3%)
  other arithmetic  71.4 us (3%)
    reduce_scatter x8, waiting for transfers between devices, collect(): return lax.psum_scatter(partial_sum, 'col', scatter_dimension=0, tiled=True)  472 us
    reduce_scatter x8, waiting for transfers between devices, collect_grad(): return lax.psum_scatter(partial_sum, 'col', scatter_dimension=0, tiled=True)  320 us
    all_gather x8, waiting for transfers between devices, spread_grad(): return lax.all_gather(shard, 'col', axis=0, tiled=True)  268 us
    all_gather x8, waiting for transfers between devices, spread(): return lax.all_gather(shard, 'col', axis=0, tiled=True)  246 us
    unnamed x47, waiting for transfers between devices  140 us
    dot_general x24, matrix products, contract_last(): lax.dot_general(left, right, (((1,), (1,)), ((), ())), preferred_element_...  114 us
    dot_general x24, matrix products, contract_first(): lax.dot_general(left, right, (((0,), (0,)), ((), ())), preferred_element_...  98.6 us
    reduce_scatter x1, waiting for transfers between devices, per_device(): lax.psum_scatter(partials[7], 'row', scatter_dimension=0, tiled=True)  79.3 us
  transfers between devices with their start and end apart: 45, of which 43 were waited for; matrix products, arithmetic and copies ran while one was open for 18% of the time, Pallas kernels for 0%

commit v1 on v0

--- a/solution.py
+++ b/solution.py
@@ -7,6 +7,19 @@
 EPSILON = 1e-05
 
 
+def collect_2(x, axis, dim):
+    ways = lax.axis_size(axis)
+    up = [(d, (d + 1) % ways) for d in range(ways)]
+    down = [(d, (d - 1) % ways) for d in range(ways)]
+    earlier, later = ([x], [x])
+    for _ in range(ways // 2):
+        earlier.append(lax.ppermute(earlier[-1], axis, up))
+    for _ in range((ways - 1) // 2):
+        later.append(lax.ppermute(later[-1], axis, down))
+    line = jnp.concatenate([*earlier[::-1], *later[1:]], axis=dim)
+    return jnp.roll(line, (lax.axis_index(axis) - ways // 2) * x.shape[dim], axis=dim)
+
+
 def contract_last(left, right):
     return lax.dot_general(
         left, right, (((1,), (1,)), ((), ())), preferred_element_type=jnp.float32
@@ -24,7 +37,7 @@
 
 
 def spread_grad(shard):
-    return lax.all_gather(shard, "col", axis=0, tiled=True)
+    return collect_2(shard, "col", 0)
 
 
 def collect(partial_sum):

time: 2560 us -> 2430 us (0.949)
  waiting for transfers between devices: 1900 us -> 1650 us
  starting transfers between devices: 4.43 us -> 97.8 us
  other arithmetic: 71.4 us -> 131 us
    all_gather x8 -> x0, waiting for transfers between devices: 268 us -> none  [spread_grad(): return lax.all_gather(shard, 'col', axis=0, tiled=True)]
    ppermute x0 -> x24, waiting for transfers between devices: none -> 202 us  [the longest x16 170 us: collect_2(): earlier.append(lax.ppermute(earlier[-1], axis, up))]
    ppermute x0 -> x24, starting transfers between devices: none -> 94.7 us  [the longest x16 81.9 us: collect_2(): earlier.append(lax.ppermute(earlier[-1], axis, up))]
    all_gather x8, waiting for transfers between devices: 246 us -> 153 us  [spread(): return lax.all_gather(shard, 'col', axis=0, tiled=True)]
    unnamed x47 -> x38, waiting for transfers between devices: 140 us -> 55.8 us
    reduce_scatter x0 -> x1, waiting for transfers between devices: none -> 79.7 us  [per_device(): lax.psum_scatter(partials[8], 'row', scatter_dimension=0, tiled=True)]
    concatenate x0 -> x8, other arithmetic: none -> 59.6 us  [collect_2(): jnp.roll(line, (lax.axis_index(axis) - ways // 2) * x.shape[dim], axis=dim)]
    reduce_scatter x8, waiting for transfers between devices: 320 us -> 264 us  [collect_grad(): return lax.psum_scatter(partial_sum, 'col', scatter_dimension=0, tiled=True)]
  transfers between devices with their start and end apart: 45 -> 61, of which waited for: 43 -> 51; matrix products, arithmetic and copies ran while one was open for 18% -> 20% of each run, Pallas kernels for 0% -> 0%
where the time goes in v1:
time: 2430 us; the launch traced here: 2420 us
  waiting for transfers between devices  1650 us (68%)
  matrix products  330 us (14%)
  other arithmetic  131 us (5%)
  local copies, waits for them, and re-layouts  116 us (5%)
  starting transfers between devices  97.8 us (4%)
  blocking collectives  74.1 us (3%)
    reduce_scatter x8, waiting for transfers between devices, collect(): return lax.psum_scatter(partial_sum, 'col', scatter_dimension=0, tiled=True)  473 us
    reduce_scatter x8, waiting for transfers between devices, collect_grad(): return lax.psum_scatter(partial_sum, 'col', scatter_dimension=0, tiled=True)  264 us
    ppermute x16, waiting for transfers between devices, collect_2(): earlier.append(lax.ppermute(earlier[-1], axis, up))  170 us
    all_gather x8, waiting for transfers between devices, spread(): return lax.all_gather(shard, 'col', axis=0, tiled=True)  153 us
    dot_general x24, matrix products, contract_first(): lax.dot_general(left, right, (((0,), (0,)), ((), ())), preferred_element_...  114 us
    dot_general x24, matrix products, contract_last(): lax.dot_general(left, right, (((1,), (1,)), ((), ())), preferred_element_...  98.1 us
    ppermute x16, starting transfers between devices, collect_2(): earlier.append(lax.ppermute(earlier[-1], axis, up))  81.9 us
    reduce_scatter x1, waiting for transfers between devices, per_device(): lax.psum_scatter(partials[8], 'row', scatter_dimension=0, tiled=True)  79.7 us
  transfers between devices with their start and end apart: 61, of which 51 were waited for; matrix products, arithmetic and copies ran while one was open for 20% of the time, Pallas kernels for 0%

profile of v1, /device:TPU:0, one launch (start us, length us, event | category | flops | bytes accessed | tf_op | source)
XLA Modules:
  0.0 2418.2 jit_solution(14620455577075247297)
XLA Ops:
  18.7 37.2 %all-gather.15.cloned.1.call-done = bf16[512,1792]{1,0:T(8,128)(2,1)} async-done(((bf16[128,1792]{1,0:T(8,128)(2,1)}), bf16[512,1792]{1,0:T(8,128)(2,1)}) %all-gather.15.cloned.1.call-update) | async-done | bytes 1835024 | tf_op jit(solution)/shard_map/all_gather | solution.py:36
  55.9 27.6 %all-gather.17.cloned.1.call-done = bf16[1792,448]{1,0:T(8,128)(2,1)} async-done(((bf16[224,448]{1,0:T(8,128)(2,1)}), bf16[1792,448]{1,0:T(8,128)(2,1)}) %all-gather.17.cloned.1.call-update) | async-done | bytes 1605648 | tf_op jit(solution)/shard_map/all_gather | solution.py:80
  190.8 36.1 %all-gather.35.cloned.1.call-done = bf16[512,1792]{1,0:T(8,128)(2,1)} async-done(((bf16[128,1792]{1,0:T(8,128)(2,1)}), bf16[512,1792]{1,0:T(8,128)(2,1)}) %all-gather.35.cloned.1.call-update) | async-done | bytes 1835024 | tf_op jit(solution)/shard_map/all_gather | solution.py:36
  338.9 71.1 %reduce-scatter.36.cloned.1.call-done = f32[128,1792]{1,0:T(8,128)} async-done(((f32[512,1792]{1,0:T(8,128)}), f32[128,1792]{1,0:T(8,128)}) %reduce-scatter.36.cloned.1.call-update) | async-done | bytes 917520 | tf_op jit(solution)/shard_map/reduce_scatter | solution.py:44
  410.0 71.0 %reduce-scatter.40.cloned.1.call-done = f32[128,1792]{1,0:T(8,128)} async-done(((f32[512,1792]{1,0:T(8,128)}), f32[128,1792]{1,0:T(8,128)}) %reduce-scatter.40.cloned.1.call-update) | async-done | bytes 917520 | tf_op jit(solution)/shard_map/reduce_scatter | solution.py:44
  481.0 71.1 %reduce-scatter.32.cloned.1.call-done = f32[128,1792]{1,0:T(8,128)} async-done(((f32[512,1792]{1,0:T(8,128)}), f32[128,1792]{1,0:T(8,128)}) %reduce-scatter.32.cloned.1.call-update) | async-done | bytes 917520 | tf_op jit(solution)/shard_map/reduce_scatter | solution.py:44
  602.9 33.4 %all-gather.37.cloned.1.call-done = bf16[512,1792]{1,0:T(8,128)(2,1)} async-done(((bf16[128,1792]{1,0:T(8,128)(2,1)}), bf16[512,1792]{1,0:T(8,128)(2,1)}) %all-gather.37.cloned.1.call-update) | async-done | bytes 1835024 | tf_op jit(solution)/shard_map/all_gather | solution.py:36
  643.0 32.2 %all-gather.27.cloned.1.call-done = bf16[1792,1216]{1,0:T(8,128)(2,1)} async-done(((bf16[224,1216]{1,0:T(8,128)(2,1)}), bf16[1792,1216]{1,0:T(8,128)(2,1)}) %all-gather.27.cloned.1.call-update) | async-done | bytes 4358160 | tf_op jit(solution)/shard_map/all_gather | solution.py:83
  682.0 33.3 %all-gather.29.cloned.1.call-done = bf16[1792,1216]{1,0:T(8,128)(2,1)} async-done(((bf16[224,1216]{1,0:T(8,128)(2,1)}), bf16[1792,1216]{1,0:T(8,128)(2,1)}) %all-gather.29.cloned.1.call-update) | async-done | bytes 4358160 | tf_op jit(solution)/shard_map/all_gather | solution.py:85
  822.6 26.4 %reduce-scatter.52.cloned.1.call-done = f32[128,1792]{1,0:T(8,128)} async-done(((f32[512,1792]{1,0:T(8,128)}), f32[128,1792]{1,0:T(8,128)}) %reduce-scatter.52.cloned.1.call-update) | async-done | bytes 917520 | tf_op jit(solution)/shard_map/reduce_scatter | solution.py:48
  849.0 70.4 %reduce-scatter.44.cloned.1.call-done = f32[128,1792]{1,0:T(8,128)} async-done(((f32[512,1792]{1,0:T(8,128)}), f32[128,1792]{1,0:T(8,128)}) %reduce-scatter.44.cloned.1.call-update) | async-done | bytes 917520 | tf_op jit(solution)/shard_map/reduce_scatter | solution.py:48
  1124.7 69.4 %reduce-scatter.56.cloned.1.call-done = f32[128,1792]{1,0:T(8,128)} async-done(((f32[512,1792]{1,0:T(8,128)}), f32[128,1792]{1,0:T(8,128)}) %reduce-scatter.56.cloned.1.call-update) | async-done | bytes 917520 | tf_op jit(solution)/shard_map/reduce_scatter | solution.py:48
  1197.9 67.4 %reduce-scatter.34.cloned.1.call-done = f32[128,1792]{1,0:T(8,128)} async-done(((f32[512,1792]{1,0:T(8,128)}), f32[128,1792]{1,0:T(8,128)}) %reduce-scatter.34.cloned.1.call-update) | async-done | bytes 917520 | tf_op jit(solution)/shard_map/reduce_scatter | solution.py:44
  1265.2 71.0 %reduce-scatter.42.cloned.1.call-done = f32[128,1792]{1,0:T(8,128)} async-done(((f32[512,1792]{1,0:T(8,128)}), f32[128,1792]{1,0:T(8,128)}) %reduce-scatter.42.cloned.1.call-update) | async-done | bytes 917520 | tf_op jit(solution)/shard_map/reduce_scatter | solution.py:44
  1531.7 50.1 %all-reduce.22.cloned.1.call-done = (bf16[32,2,448]{2,0,1:T(8,128)(2,1)}, bf16[32,2,448]{2,0,1:T(8,128)(2,1)}, bf16[32,2,448]{2,0,1:T(8,128)(2,1)}, bf16[32,2,448]{2,0,1:T(8,128)(2,1)}) async-done(((bf16[32,2,448]{2,0,1:T(8,128)(2,1)}, bf16[32,2,448]{2,0,1:T(8,128)(2,1)}, bf16[32,2,448]{2,0,1:T(8,128)(2,1)}, bf16[32,2,448]{2,0,1:T(8,128)(2,1)}), (bf16[32,2,448]{2,0,1:T(8,128)(2,1)}, ...) | async-done | bytes 229392
  1799.8 71.2 %reduce-scatter.46.cloned.1.call-done = f32[128,1792]{1,0:T(8,128)} async-done(((f32[512,1792]{1,0:T(8,128)}), f32[128,1792]{1,0:T(8,128)}) %reduce-scatter.46.cloned.1.call-update) | async-done | bytes 917520 | tf_op jit(solution)/shard_map/reduce_scatter | solution.py:48
  1913.0 29.4 %reduce-scatter.38.cloned.1.call-done = f32[128,1792]{1,0:T(8,128)} async-done(((f32[512,1792]{1,0:T(8,128)}), f32[128,1792]{1,0:T(8,128)}) %reduce-scatter.38.cloned.1.call-update) | async-done | bytes 917520 | tf_op jit(solution)/shard_map/reduce_scatter | solution.py:44
  1946.0 67.6 %reduce-scatter.30.cloned.1.call-done = f32[128,1792]{1,0:T(8,128)} async-done(((f32[512,1792]{1,0:T(8,128)}), f32[128,1792]{1,0:T(8,128)}) %reduce-scatter.30.cloned.1.call-update) | async-done | bytes 917520 | tf_op jit(solution)/shard_map/reduce_scatter | solution.py:44
  2023.9 69.8 %reduce-scatter.66.cloned.1.call-done = f32[224,1216]{1,0:T(8,128)} async-done(((f32[1792,1216]{1,0:T(8,128)}), f32[224,1216]{1,0:T(8,128)}) %reduce-scatter.66.cloned.1.call-update) | async-done | bytes 1089552 | tf_op jit(solution)/shard_map/reduce_scatter | solution.py:209
  2093.7 79.1 %reduce-scatter.68.cloned.1.call-done = f32[224,1216]{1,0:T(8,128)} async-done(((f32[1792,1216]{1,0:T(8,128)}), f32[224,1216]{1,0:T(8,128)}) %reduce-scatter.68.cloned.1.call-update) | async-done | bytes 1089552 | tf_op jit(solution)/shard_map/reduce_scatter | solution.py:210
  2172.8 79.7 %reduce-scatter.70.cloned.1.call-done = f32[224,1216]{1,0:T(8,128)} async-done(((f32[1792,1216]{1,0:T(8,128)}), f32[224,1216]{1,0:T(8,128)}) %reduce-scatter.70.cloned.1.call-update) | async-done | bytes 1089552 | tf_op jit(solution)/shard_map/reduce_scatter | solution.py:211
  2252.5 52.8 %reduce-scatter.62.cloned.1.call-done = f32[224,448]{1,0:T(8,128)} async-done(((f32[1792,448]{1,0:T(8,128)}), f32[224,448]{1,0:T(8,128)}) %reduce-scatter.62.cloned.1.call-update) | async-done | bytes 401424 | tf_op jit(solution)/shard_map/reduce_scatter | solution.py:205
  2305.3 53.0 %reduce-scatter.64.cloned.1.call-done = f32[224,448]{1,0:T(8,128)} async-done(((f32[1792,448]{1,0:T(8,128)}), f32[224,448]{1,0:T(8,128)}) %reduce-scatter.64.cloned.1.call-update) | async-done | bytes 401424 | tf_op jit(solution)/shard_map/reduce_scatter | solution.py:207
  2358.3 52.6 %reduce-scatter.60.cloned.1.call-done = f32[224,448]{1,0:T(8,128)} async-done(((f32[1792,448]{1,0:T(8,128)}), f32[224,448]{1,0:T(8,128)}) %reduce-scatter.60.cloned.1.call-update) | async-done | bytes 401424 | tf_op jit(solution)/shard_map/reduce_scatter | solution.py:204
  (840 shorter events, 1074.9 us)
Async XLA Ops:
  14.3 212.6 %all-gather.35.cloned.1.call-start = ((), (), s32[]{:S(2)}) async-start(), calls=%async_computation.36 | async-start | bytes 2293760 | tf_op jit(solution)/shard_map/all_gather | solution.py:36
  14.9 253.9 %all-gather.39.cloned.1.call-start = ((), (), s32[]{:S(2)}) async-start(), calls=%async_computation.40 | async-start | bytes 2293760 | tf_op jit(solution)/shard_map/all_gather | solution.py:36
  15.6 323.3 %reduce-scatter.28.cloned.1.call-start = ((), (), s32[]{:S(2)}) async-start(), calls=%async_computation.26 | async-start | bytes 4587520 | tf_op jit(solution)/shard_map/reduce_scatter | solution.py:44
  188.1 221.9 %reduce-scatter.36.cloned.1.call-start = ((), (), s32[]{:S(2)}) async-start(), calls=%async_computation.37 | async-start | bytes 4587520 | tf_op jit(solution)/shard_map/reduce_scatter | solution.py:44
  310.5 241.6 %reduce-scatter.32.cloned.1.call-start = ((), (), s32[]{:S(2)}) async-start(), calls=%async_computation.33 | async-start | bytes 4587520 | tf_op jit(solution)/shard_map/reduce_scatter | solution.py:44
  313.6 289.2 %all-gather.25.cloned.1.call-start = ((), (), s32[]{:S(2)}) async-start(), calls=%async_computation.28 | async-start | bytes 5160960 | tf_op jit(solution)/shard_map/all_gather | solution.py:82
  314.2 322.0 %all-gather.37.cloned.1.call-start = ((), (), s32[]{:S(2)}) async-start(), calls=%async_computation.38 | async-start | bytes 2293760 | tf_op jit(solution)/shard_map/all_gather | solution.py:36
  559.7 237.1 %all-gather.23.cloned.1.call-start = ((), (), s32[]{:S(2)}) async-start(), calls=%async_computation.27 | async-start | bytes 2293760 | tf_op jit(solution)/shard_map/all_gather | solution.py:36
  602.4 246.6 %reduce-scatter.52.cloned.1.call-start = ((), (), s32[]{:S(2)}) async-start(), calls=%async_computation.48 | async-start | bytes 4587520 | tf_op jit(solution)/shard_map/reduce_scatter | solution.py:48
  734.9 184.5 %reduce-scatter.44.cloned.1.call-start = ((), (), s32[]{:S(2)}) async-start(), calls=%async_computation.44 | async-start | bytes 4587520 | tf_op jit(solution)/shard_map/reduce_scatter | solution.py:48
  1109.0 227.3 %reduce-scatter.42.cloned.1.call-start = ((), (), s32[]{:S(2)}) async-start(), calls=%async_computation.43 | async-start | bytes 4587520 | tf_op jit(solution)/shard_map/reduce_scatter | solution.py:44
  1116.3 465.5 %all-reduce.22.cloned.1.call-start = ((), (), s32[]{:S(2)}) async-start(), calls=%async_computation.58 | async-start | bytes 524288
  1529.2 252.1 %reduce-scatter.54.cloned.1.call-start = ((), (), s32[]{:S(2)}) async-start(), calls=%async_computation.49 | async-start | bytes 4587520 | tf_op jit(solution)/shard_map/reduce_scatter | solution.py:48
  1589.6 191.7 %reduce-scatter.58.cloned.1.call-start = ((), (), s32[]{:S(2)}) async-start(), calls=%async_computation.51 | async-start | bytes 4587520 | tf_op jit(solution)/shard_map/reduce_scatter | solution.py:48
  1607.3 192.5 %reduce-scatter.50.cloned.1.call-start = ((), (), s32[]{:S(2)}) async-start(), calls=%async_computation.47 | async-start | bytes 4587520 | tf_op jit(solution)/shard_map/reduce_scatter | solution.py:48
  1624.7 246.3 %reduce-scatter.46.cloned.1.call-start = ((), (), s32[]{:S(2)}) async-start(), calls=%async_computation.45 | async-start | bytes 4587520 | tf_op jit(solution)/shard_map/reduce_scatter | solution.py:48
  1639.4 302.9 %reduce-scatter.38.cloned.1.call-start = ((), (), s32[]{:S(2)}) async-start(), calls=%async_computation.39 | async-start | bytes 4587520 | tf_op jit(solution)/shard_map/reduce_scatter | solution.py:44
  1647.5 366.0 %reduce-scatter.30.cloned.1.call-start = ((), (), s32[]{:S(2)}) async-start(), calls=%async_computation.31 | async-start | bytes 4587520 | tf_op jit(solution)/shard_map/reduce_scatter | solution.py:44
  1655.6 438.1 %reduce-scatter.66.cloned.1.call-start = ((), (), s32[]{:S(2)}) async-start(), calls=%async_computation.55 | async-start | bytes 10321920 | tf_op jit(solution)/shard_map/reduce_scatter | solution.py:209
  1686.4 486.4 %reduce-scatter.68.cloned.1.call-start = ((), (), s32[]{:S(2)}) async-start(), calls=%async_computation.56 | async-start | bytes 10321920 | tf_op jit(solution)/shard_map/reduce_scatter | solution.py:210
  1716.5 536.0 %reduce-scatter.70.cloned.1.call-start = ((), (), s32[]{:S(2)}) async-start(), calls=%async_computation.57 | async-start | bytes 10321920 | tf_op jit(solution)/shard_map/reduce_scatter | solution.py:211
  1748.3 557.0 %reduce-scatter.62.cloned.1.call-start = ((), (), s32[]{:S(2)}) async-start(), calls=%async_computation.53 | async-start | bytes 4128768 | tf_op jit(solution)/shard_map/reduce_scatter | solution.py:205
  1758.3 600.0 %reduce-scatter.64.cloned.1.call-start = ((), (), s32[]{:S(2)}) async-start(), calls=%async_computation.54 | async-start | bytes 4128768 | tf_op jit(solution)/shard_map/reduce_scatter | solution.py:207
  1768.5 642.4 %reduce-scatter.60.cloned.1.call-start = ((), (), s32[]{:S(2)}) async-start(), calls=%async_computation.52 | async-start | bytes 4128768 | tf_op jit(solution)/shard_map/reduce_scatter | solution.py:204
  (259 other events, 11069.7 us)
Sparse Core Ops, SparseCore 0:
  271.6 67.2 reduce-scatter.27
  341.2 68.7 reduce-scatter.35
  412.2 68.7 reduce-scatter.39
  483.3 68.7 reduce-scatter.31
  717.4 60.4 all-gather.22
  780.5 68.4 reduce-scatter.51
  851.2 68.2 reduce-scatter.43
  924.0 63.6 all-gather.32
  989.1 62.7 all-gather.40
  1054.7 69.9 reduce-scatter.47
  1127.0 67.0 reduce-scatter.55
  1196.4 68.7 reduce-scatter.33
  1267.4 68.7 reduce-scatter.41
  1529.3 52.4 all-reduce.21
  1589.7 67.7 reduce-scatter.53
  1659.8 68.7 reduce-scatter.57
  1731.0 68.7 reduce-scatter.49
  1802.2 68.7 reduce-scatter.45
  1873.3 69.0 reduce-scatter.37
  1944.8 68.7 reduce-scatter.29
  2018.2 75.4 reduce-scatter.65
  2097.7 75.0 reduce-scatter.67
  2177.5 75.0 reduce-scatter.69
  2362.2 48.7 reduce-scatter.59
  (13 shorter events, 498.0 us)
